TPU v7x, 512 devices: a whole 4x4x16 slice. The times are simulated.
512 devices in a mesh: line: 32 (over x, y, core), seg: 16 (over z).
Axes of the slice: x: 4, y: 4, z: 16, core: 2. Of those that a mesh axis runs over, the one named last changes fastest.
Arguments:
- points: float32 [32, 16, 3, 32768], P('line', 'seg'), may hold values from -1 to 1
- rows: int32 [32, 16, 2, 3072], P('line', 'seg'), may hold values from -1 to 32767, as said below
- cells: int32 [32, 16, 2, 24], P('line', 'seg'), may hold values from -1 to 15, as said below
- pose: float32 [12, 32], P(None, 'line'), as said below
Outputs:
- matched: float32 [32, 16, 2, 5, 3072], P('line', 'seg')
- fitted_pose: float32 [12, 32], P(None, 'line')
- final_spread: float32 [1], replicated
Inputs may be any that keep to these rules, and one draw needn't show every extreme that they name: In each block of 128 slots the filled slots come first; every slot of an empty block is empty; rows toward the lower line lie in the lower margin (below 8192), rows toward the upper line in the upper margin (24576 or more); the lists of line 0 toward the lower side and of line 32 - 1 toward the upper side are empty. `cells`: empty blocks come after the others; in segment 0 of every line all blocks toward an existing adjacent line are filled. `pose`: every 3x3 part is within about 0.5 of the identity.
All inputs are finite; a program needn't handle non-finite values.
Results may differ from a plain program's by a relative error of at most 0.0003.
Values sent between devices are 32-bit elements; how exact they have to be, the bound alone decides.
A program may use at most 64 MiB of HBM per device.

v0:
```python
import jax
import jax.numpy as jnp
from jax import lax
from jax.sharding import PartitionSpec as P

NCELL = 16
CT = 512
BLOCK = 128
ITERS = 2


OUTLIER_MASS = 1.0
SPREAD_START = 0.05
PRIOR_TOP = 0.05
PRIOR_BOTTOM = 1.0
REGULARIZE = 1.0
blocks_per_turn = 4


def from_behind(value, axis, steps):
    count = lax.axis_size(axis)
    initial, last = (max(0, -steps), min(count, count - steps))
    return lax.ppermute(value, axis, [(source, source + steps) for source in range(initial, last)])


def match_block(source_block, cell_id, world_points, spread):
    first_column = jnp.maximum(cell_id, 0) * CT
    target = lax.dynamic_slice_in_dim(world_points, first_column, CT, 1)
    distance = (source_block[0][:, None] - target[0][None, :]) ** 2
    distance = distance + (source_block[1][:, None] - target[1][None, :]) ** 2
    distance = distance + (source_block[2][:, None] - target[2][None, :]) ** 2
    weight = jnp.exp(-distance / (2.0 * spread))
    total_weight = jnp.sum(weight, axis=1)
    posterior = weight / (total_weight + OUTLIER_MASS)[:, None]
    pulled = lax.dot_general(
        target,
        posterior,
        (((1,), (1,)), ((), ())),
        precision=lax.Precision.HIGHEST,
        preferred_element_type=jnp.float32,
    )
    share_row = total_weight / (total_weight + OUTLIER_MASS)
    energy_row = jnp.sum(posterior * distance, axis=1)
    merged_rows = jnp.concatenate([pulled, share_row[None, :], energy_row[None, :]], axis=0)
    return jnp.where(cell_id >= 0, merged_rows, jnp.zeros_like(merged_rows))


def match_all(sources, block_cells, worlds, spread):
    block_total = block_cells.shape[1]
    turns = 2 * block_total // blocks_per_turn
    grouped = (
        sources.reshape(2, 3, block_total, BLOCK)
        .transpose(0, 2, 1, 3)
        .reshape(turns, blocks_per_turn, 3, BLOCK)
    )
    grouped_cells = block_cells.reshape(turns, blocks_per_turn)
    sides = jnp.arange(turns) // (turns // 2)

    def one_turn(packed):
        turn_blocks, turn_cells, side = packed
        target_world = lax.dynamic_index_in_dim(worlds, side, 0, keepdims=False)

        def compute(unused):
            return jax.vmap(
                lambda block_points, block_cell: match_block(
                    block_points, block_cell, target_world, spread
                )
            )(turn_blocks, turn_cells)

        def skipped(unused):
            return jnp.zeros((blocks_per_turn, 5, BLOCK), jnp.float32)

        return lax.cond(jnp.any(turn_cells >= 0), compute, skipped, 0)

    output = lax.map(one_turn, (grouped, grouped_cells, sides))
    return (
        output.reshape(2, block_total, 5, BLOCK)
        .transpose(0, 2, 1, 3)
        .reshape(2, 5, block_total * BLOCK)
    )


def solve_pose(gram_matrix, cross_matrix, pose_column):
    old_pose = jnp.concatenate(
        [pose_column[:9].reshape(3, 3), pose_column[9:].reshape(3, 1)], axis=1
    )
    left_side = gram_matrix + REGULARIZE * jnp.eye(4, dtype=gram_matrix.dtype)
    right_side = cross_matrix + REGULARIZE * old_pose
    factor = jnp.linalg.cholesky(left_side)
    solved = jax.scipy.linalg.cho_solve((factor, True), right_side.T)
    new_pose = solved.T
    return jnp.concatenate([new_pose[:, :3].reshape(9), new_pose[:, 3]])


def send_lists(lists, marks, step):
    return from_behind((lists, marks), "line", step)


def send_back(piece, step):
    return from_behind(piece, "line", step)


def on_device(points, rows, cells, pose):
    own_points = points[0, 0]
    row_list = rows[0, 0]
    cell_ids = cells[0, 0]
    pose_column = pose[:, 0]
    margin = NCELL * CT
    point_total = own_points.shape[1]
    slot_total = row_list.shape[1]
    live_slots = (row_list >= 0).astype(jnp.float32)
    safe_rows = jnp.where(row_list >= 0, row_list, 0)
    raw_source = (
        jnp.take(own_points, safe_rows.reshape(-1), axis=1)
        .reshape(3, 2, slot_total)
        .transpose(1, 0, 2)
    )
    extended = jnp.concatenate([raw_source, jnp.ones((2, 1, slot_total), jnp.float32)], axis=1)
    spread = jnp.float32(SPREAD_START)
    result = None
    for iteration in range(ITERS):
        linear_part = pose_column[:9].reshape(3, 3)
        offset_part = pose_column[9:]
        world_points = (
            jnp.dot(
                linear_part,
                own_points,
                precision=lax.Precision.HIGHEST,
                preferred_element_type=jnp.float32,
            )
            + offset_part[:, None]
        )
        moved_source = (
            jnp.einsum("km,dms->dks", linear_part, raw_source, precision=lax.Precision.HIGHEST)
            + offset_part[None, :, None]
        )
        lower_margin = world_points[:, :margin]
        upper_margin = world_points[:, point_total - margin :]
        cell_marks = (cell_ids + 1).astype(jnp.float32)
        lists_down, marks_down = send_lists(moved_source[0], cell_marks[0], -1)
        lists_up, marks_up = send_lists(moved_source[1], cell_marks[1], 1)
        incoming = jnp.stack([lists_down, lists_up])
        got_cells = jnp.stack([marks_down, marks_up]).astype(jnp.int32) - 1
        own_worlds = jnp.stack([upper_margin, lower_margin])
        answers = match_all(incoming, got_cells, own_worlds, spread)
        result = jnp.stack([send_back(answers[0], 1), send_back(answers[1], -1)])
        result = result * live_slots[:, None, :]
        pulled = result[:, :3]
        share_all = result[:, 3]
        energy_all = result[:, 4]
        gram_matrix = jnp.einsum(
            "dks,dms->km",
            extended * share_all[:, None, :],
            extended,
            precision=lax.Precision.HIGHEST,
        )
        cross_matrix = jnp.einsum("dks,dms->km", pulled, extended, precision=lax.Precision.HIGHEST)
        energy_part = jnp.sum(energy_all)
        share_part = jnp.sum(share_all)
        gram_sum, cross_sum = lax.psum((gram_matrix, cross_matrix), "seg")
        energy_sum, share_sum = lax.psum((energy_part, share_part), ("line", "seg"))
        pose_column = solve_pose(gram_sum, cross_sum, pose_column)
        spread = (energy_sum + PRIOR_TOP) / (3.0 * share_sum + PRIOR_BOTTOM)
    return (result[None, None], pose_column[:, None], spread.reshape(1))


def solution(mesh):
    return jax.shard_map(
        on_device,
        mesh=mesh,
        in_specs=(
            P("line", "seg", None, None),
            P("line", "seg", None, None),
            P("line", "seg", None, None),
            P(None, "line"),
        ),
        out_specs=(P("line", "seg", None, None, None), P(None, "line"), P()),
        check_vma=False,
    )
```

profile of v0, /device:TPU:1, one launch (start us, length us, event | category | flops | bytes accessed | tf_op | source)
XLA Modules:
  0.0 665.1 jit_solution(6395573650611481252)
XLA Ops:
  13.1 21.8 %gather_fusion = f32[6144,3]{1,0:T(8,128)S(1)} fusion(f32[3,32768]{0,1:T(8,128)} %bitcast.285, s32[6144]{0:T(1024)S(1)} %broadcast_clamp_fusion), kind=kCustom, calls=%fused_computation | custom fusion | bytes 172032 | tf_op jit(solution)/shard_map/jit(_take)/gather | solution.py:114
  52.3 16.7 %convolution_add_fusion.1 = f32[3,32768]{1,0:T(4,128)S(1)} fusion(f32[3,3]{1,0:T(4,128)S(1)} %reshape.263, f32[3]{0:T(128)S(1)} %get-tuple-element.442, f32[1,1,3,32768]{2,3,1,0:T(8,128)} %copy.18), kind=kOutput, calls=%fused_computation.61 | convolution fusion | flops 3637248 | bytes 786480 | tf_op jit(solution)/shard_map/dot_general | solution.py:125
  69.4 139.7 %while.28 = (s32[]{:T(128)}, f32[12,4,5,128]{3,2,1,0:T(8,128)S(1)}, s32[12,4]{1,0:T(8,128)S(1)}, f32[2,3,8192]{2,1,0:T(4,128)S(1)}, f32[12,4,3,128]{3,1,2,0:T(4,128)S(1)}, /*index=5*/s32[]{:T(128)}, s32[]{:T(128)}, s32[]{:T(128)}) while((s32[]{:T(128)}, f32[12,4,5,128]{3,2,1,0:T(8,128)S(1)}, s32[12,4]{1,0:T(8,128)S(1)}, ...), condition=%wide.region_6.7_spmd.clone, body=%wide.region_0.6_spmd.clone.sunk | while | flops 18620548 | bytes 529362 | solution.py:75
  70.7 10.3 %conditional.6 = (f32[1,4,5,128]{3,2,1,0:T(8,128)S(1)}) conditional(s32[]{:T(128)} %convert_element_type.49, () %tuple.138, (s32[4]{0:T(128)S(1)}, s32[12]{0:T(128)S(1)}, s32[]{:T(128)}, f32[2,3,8192]{2,1,0:T(4,128)S(1)}, f32[12,4,3,128]{3,1,2,0:T(4,128)S(1)}, /*index=5*/s32[12]{0:T(128)S(1)}, s32[12]{0:T(128)S(1)}, s32[12]{0:T(128)S(1)}, ...), branch_computations={%region_2.2_spmd, %region_3.5_spmd.clone} | conditional | flops 18620528 | bytes 496227 | solution.py:73
  105.6 10.3 %conditional.6 = (f32[1,4,5,128]{3,2,1,0:T(8,128)S(1)}) conditional(s32[]{:T(128)} %convert_element_type.49, () %tuple.138, (s32[4]{0:T(128)S(1)}, s32[12]{0:T(128)S(1)}, s32[]{:T(128)}, f32[2,3,8192]{2,1,0:T(4,128)S(1)}, f32[12,4,3,128]{3,1,2,0:T(4,128)S(1)}, /*index=5*/s32[12]{0:T(128)S(1)}, s32[12]{0:T(128)S(1)}, s32[12]{0:T(128)S(1)}, ...), branch_computations={%region_2.2_spmd, %region_3.5_spmd.clone} | conditional | flops 18620528 | bytes 496227 | solution.py:73
  128.9 10.3 %conditional.6 = (f32[1,4,5,128]{3,2,1,0:T(8,128)S(1)}) conditional(s32[]{:T(128)} %convert_element_type.49, () %tuple.138, (s32[4]{0:T(128)S(1)}, s32[12]{0:T(128)S(1)}, s32[]{:T(128)}, f32[2,3,8192]{2,1,0:T(4,128)S(1)}, f32[12,4,3,128]{3,1,2,0:T(4,128)S(1)}, /*index=5*/s32[12]{0:T(128)S(1)}, s32[12]{0:T(128)S(1)}, s32[12]{0:T(128)S(1)}, ...), branch_computations={%region_2.2_spmd, %region_3.5_spmd.clone} | conditional | flops 18620528 | bytes 496227 | solution.py:73
  219.0 20.4 %all-reduce.6 = (f32[3,4]{1,0:T(4,128)S(1)}, f32[4,4]{0,1:T(4,128)S(1)}) all-reduce(f32[3,4]{1,0:T(4,128)S(1)} %convolution_bitcast_fusion.6, f32[4,4]{0,1:T(4,128)S(1)} %convolution_bitcast_fusion.7), channel_id=1, replica_groups=mesh['line'=32,'seg'=16] {'seg'}, use_global_device_ids=true, to_apply=%region_10.12 | all-reduce | flops 28 | bytes 224 | tf_op jit(solution)/shard_map/psum | solution.py:160
  242.3 16.7 %convolution_add_fusion = f32[3,32768]{1,0:T(4,128)S(1)} fusion(f32[3]{0:T(128)S(1)} %slice_reduce_fusion.3, f32[3,4]{1,0:T(4,128)S(1)} %convolution_bitcast_fusion.5, f32[1,1,3,32768]{2,3,1,0:T(8,128)} %copy.18), kind=kOutput, calls=%fused_computation.60 | convolution fusion | flops 3637248 | bytes 786492 | tf_op jit(solution)/shard_map/dot_general | solution.py:125
  269.8 111.2 %all-reduce.4 = (f32[]{:T(128)}, f32[]{:T(128)}) all-reduce(f32[]{:T(128)} %get-tuple-element.356, f32[]{:T(128)} %get-tuple-element.355), channel_id=1, replica_groups=mesh['line'=32,'seg'=16] {'line','seg'}, use_global_device_ids=true, to_apply=%region_12.15 | all-reduce | flops 2 | bytes 16 | tf_op jit(solution)/shard_map/psum | solution.py:161
  382.5 140.6 %while.29 = (s32[]{:T(128)}, f32[12,4,5,128]{3,2,1,0:T(8,128)S(1)}, s32[12,4]{1,0:T(8,128)S(1)}, f32[2,3,8192]{2,1,0:T(4,128)S(1)}, f32[12,4,3,128]{3,1,2,0:T(4,...) while((s32[]{:T(128)}, f32[12,4,5,128]{3,2,1,0:T(8,128)S(1)}, ...), condition=%wide.region_21.24_spmd.clone, body=%wide.region_15.23_spmd.clone.sunk | while | flops 18620552 | bytes 529402 | solution.py:75
  383.8 10.4 %conditional.7 = (f32[1,4,5,128]{3,2,1,0:T(8,128)S(1)}) conditional(s32[]{:T(128)} %convert_element_type.50, () %tuple.142, (s32[4]{0:T(128)S(1)}, s32[12]{0:T(128)S(1)}, s32[]{:T(128)}, f32[2,3,8192]{2,1,0:T(4,128)S(1)}, f32[12,4,3,128]{3,1,2,0:T(4,128)S(1)}, /*index=5*/f32[]{:T(128)}, s32[12]{0:T(128)S(1)}, s32[12]{0:T(128)S(1)}, ...), branch_computations={%region_17.19_spmd, %region_18.22_spmd.clone} | conditional | flops 18620530 | bytes 496251 | solution.py:73
  395.5 10.4 %conditional.7 = (f32[1,4,5,128]{3,2,1,0:T(8,128)S(1)}) conditional(s32[]{:T(128)} %convert_element_type.50, () %tuple.142, (s32[4]{0:T(128)S(1)}, s32[12]{0:T(128)S(1)}, s32[]{:T(128)}, f32[2,3,8192]{2,1,0:T(4,128)S(1)}, f32[12,4,3,128]{3,1,2,0:T(4,128)S(1)}, /*index=5*/f32[]{:T(128)}, s32[12]{0:T(128)S(1)}, s32[12]{0:T(128)S(1)}, ...), branch_computations={%region_17.19_spmd, %region_18.22_spmd.clone} | conditional | flops 18620530 | bytes 496251 | solution.py:73
  407.2 10.4 %conditional.7 = (f32[1,4,5,128]{3,2,1,0:T(8,128)S(1)}) conditional(s32[]{:T(128)} %convert_element_type.50, () %tuple.142, (s32[4]{0:T(128)S(1)}, s32[12]{0:T(128)S(1)}, s32[]{:T(128)}, f32[2,3,8192]{2,1,0:T(4,128)S(1)}, f32[12,4,3,128]{3,1,2,0:T(4,128)S(1)}, /*index=5*/f32[]{:T(128)}, s32[12]{0:T(128)S(1)}, s32[12]{0:T(128)S(1)}, ...), branch_computations={%region_17.19_spmd, %region_18.22_spmd.clone} | conditional | flops 18620530 | bytes 496251 | solution.py:73
  418.9 10.4 %conditional.7 = (f32[1,4,5,128]{3,2,1,0:T(8,128)S(1)}) conditional(s32[]{:T(128)} %convert_element_type.50, () %tuple.142, (s32[4]{0:T(128)S(1)}, s32[12]{0:T(128)S(1)}, s32[]{:T(128)}, f32[2,3,8192]{2,1,0:T(4,128)S(1)}, f32[12,4,3,128]{3,1,2,0:T(4,128)S(1)}, /*index=5*/f32[]{:T(128)}, s32[12]{0:T(128)S(1)}, s32[12]{0:T(128)S(1)}, ...), branch_computations={%region_17.19_spmd, %region_18.22_spmd.clone} | conditional | flops 18620530 | bytes 496251 | solution.py:73
  430.6 10.4 %conditional.7 = (f32[1,4,5,128]{3,2,1,0:T(8,128)S(1)}) conditional(s32[]{:T(128)} %convert_element_type.50, () %tuple.142, (s32[4]{0:T(128)S(1)}, s32[12]{0:T(128)S(1)}, s32[]{:T(128)}, f32[2,3,8192]{2,1,0:T(4,128)S(1)}, f32[12,4,3,128]{3,1,2,0:T(4,128)S(1)}, /*index=5*/f32[]{:T(128)}, s32[12]{0:T(128)S(1)}, s32[12]{0:T(128)S(1)}, ...), branch_computations={%region_17.19_spmd, %region_18.22_spmd.clone} | conditional | flops 18620530 | bytes 496251 | solution.py:73
  442.3 10.4 %conditional.7 = (f32[1,4,5,128]{3,2,1,0:T(8,128)S(1)}) conditional(s32[]{:T(128)} %convert_element_type.50, () %tuple.142, (s32[4]{0:T(128)S(1)}, s32[12]{0:T(128)S(1)}, s32[]{:T(128)}, f32[2,3,8192]{2,1,0:T(4,128)S(1)}, f32[12,4,3,128]{3,1,2,0:T(4,128)S(1)}, /*index=5*/f32[]{:T(128)}, s32[12]{0:T(128)S(1)}, s32[12]{0:T(128)S(1)}, ...), branch_computations={%region_17.19_spmd, %region_18.22_spmd.clone} | conditional | flops 18620530 | bytes 496251 | solution.py:73
  454.0 10.4 %conditional.7 = (f32[1,4,5,128]{3,2,1,0:T(8,128)S(1)}) conditional(s32[]{:T(128)} %convert_element_type.50, () %tuple.142, (s32[4]{0:T(128)S(1)}, s32[12]{0:T(128)S(1)}, s32[]{:T(128)}, f32[2,3,8192]{2,1,0:T(4,128)S(1)}, f32[12,4,3,128]{3,1,2,0:T(4,128)S(1)}, /*index=5*/f32[]{:T(128)}, s32[12]{0:T(128)S(1)}, s32[12]{0:T(128)S(1)}, ...), branch_computations={%region_17.19_spmd, %region_18.22_spmd.clone} | conditional | flops 18620530 | bytes 496251 | solution.py:73
  465.8 10.4 %conditional.7 = (f32[1,4,5,128]{3,2,1,0:T(8,128)S(1)}) conditional(s32[]{:T(128)} %convert_element_type.50, () %tuple.142, (s32[4]{0:T(128)S(1)}, s32[12]{0:T(128)S(1)}, s32[]{:T(128)}, f32[2,3,8192]{2,1,0:T(4,128)S(1)}, f32[12,4,3,128]{3,1,2,0:T(4,128)S(1)}, /*index=5*/f32[]{:T(128)}, s32[12]{0:T(128)S(1)}, s32[12]{0:T(128)S(1)}, ...), branch_computations={%region_17.19_spmd, %region_18.22_spmd.clone} | conditional | flops 18620530 | bytes 496251 | solution.py:73
  477.5 10.4 %conditional.7 = (f32[1,4,5,128]{3,2,1,0:T(8,128)S(1)}) conditional(s32[]{:T(128)} %convert_element_type.50, () %tuple.142, (s32[4]{0:T(128)S(1)}, s32[12]{0:T(128)S(1)}, s32[]{:T(128)}, f32[2,3,8192]{2,1,0:T(4,128)S(1)}, f32[12,4,3,128]{3,1,2,0:T(4,128)S(1)}, /*index=5*/f32[]{:T(128)}, s32[12]{0:T(128)S(1)}, s32[12]{0:T(128)S(1)}, ...), branch_computations={%region_17.19_spmd, %region_18.22_spmd.clone} | conditional | flops 18620530 | bytes 496251 | solution.py:73
  489.2 10.4 %conditional.7 = (f32[1,4,5,128]{3,2,1,0:T(8,128)S(1)}) conditional(s32[]{:T(128)} %convert_element_type.50, () %tuple.142, (s32[4]{0:T(128)S(1)}, s32[12]{0:T(128)S(1)}, s32[]{:T(128)}, f32[2,3,8192]{2,1,0:T(4,128)S(1)}, f32[12,4,3,128]{3,1,2,0:T(4,128)S(1)}, /*index=5*/f32[]{:T(128)}, s32[12]{0:T(128)S(1)}, s32[12]{0:T(128)S(1)}, ...), branch_computations={%region_17.19_spmd, %region_18.22_spmd.clone} | conditional | flops 18620530 | bytes 496251 | solution.py:73
  500.9 10.4 %conditional.7 = (f32[1,4,5,128]{3,2,1,0:T(8,128)S(1)}) conditional(s32[]{:T(128)} %convert_element_type.50, () %tuple.142, (s32[4]{0:T(128)S(1)}, s32[12]{0:T(128)S(1)}, s32[]{:T(128)}, f32[2,3,8192]{2,1,0:T(4,128)S(1)}, f32[12,4,3,128]{3,1,2,0:T(4,128)S(1)}, /*index=5*/f32[]{:T(128)}, s32[12]{0:T(128)S(1)}, s32[12]{0:T(128)S(1)}, ...), branch_computations={%region_17.19_spmd, %region_18.22_spmd.clone} | conditional | flops 18620530 | bytes 496251 | solution.py:73
  512.6 10.4 %conditional.7 = (f32[1,4,5,128]{3,2,1,0:T(8,128)S(1)}) conditional(s32[]{:T(128)} %convert_element_type.50, () %tuple.142, (s32[4]{0:T(128)S(1)}, s32[12]{0:T(128)S(1)}, s32[]{:T(128)}, f32[2,3,8192]{2,1,0:T(4,128)S(1)}, f32[12,4,3,128]{3,1,2,0:T(4,128)S(1)}, /*index=5*/f32[]{:T(128)}, s32[12]{0:T(128)S(1)}, s32[12]{0:T(128)S(1)}, ...), branch_computations={%region_17.19_spmd, %region_18.22_spmd.clone} | conditional | flops 18620530 | bytes 496251 | solution.py:73
  532.6 102.5 %all-reduce.3 = (f32[]{:T(128)}, f32[]{:T(128)}) all-reduce(f32[]{:T(128)} %get-tuple-element.354, f32[]{:T(128)} %get-tuple-element.353), channel_id=1, replica_groups=mesh['line'=32,'seg'=16] {'line','seg'}, use_global_device_ids=true, to_apply=%region_25.28 | all-reduce | flops 2 | bytes 16 | tf_op jit(solution)/shard_map/psum | solution.py:161
  636.9 22.8 %all-reduce.5 = (f32[4,4]{0,1:T(4,128)S(1)}, f32[3,4]{1,0:T(4,128)S(1)}) all-reduce(f32[4,4]{0,1:T(4,128)S(1)} %convolution_bitcast_fusion.4, f32[3,4]{1,0:T(4,128)S(1)} %convolution_bitcast_fusion.3), channel_id=1, replica_groups=mesh['line'=32,'seg'=16] {'seg'}, use_global_device_ids=true, to_apply=%region_22.25 | all-reduce | flops 28 | bytes 224 | tf_op jit(solution)/shard_map/psum | solution.py:160
  (973 shorter events, 499.8 us)
Async XLA Ops:
  0.6 46.0 %copy-start = (s32[1,1,2,24]{3,2,1,0:T(2,128)S(1)}, s32[1,1,2,24]{3,2,1,0:T(2,128)}, u32[]{:S(2)}) copy-start(s32[1,1,2,24]{3,2,1,0:T(2,128)} %param.17) | copy-start | bytes 580
  36.6 32.7 %collective-permute-start.3 = (f32[3,3072]{1,0:T(4,128)S(1)}, f32[3,3072]{1,0:T(4,128)S(1)}, u32[]{:S(2)}, u32[]{:S(2)}) collective-permute-start(f32[3,3072]{1,0:T(4,128)S(1)} %get-tuple-element.436), channel_id=1, source_target_pairs={{0,16},{16,32},{32,48},{48,64},{64,80},{80,96},{96,112},{112,128},... | collective-permute-start | bytes 110600 | tf_op jit(solution)/shard_map/ppermute | solution.py:23
  41.1 28.1 %collective-permute-start.2 = (f32[3,3072]{1,0:T(4,128)S(1)}, f32[3,3072]{1,0:T(4,128)S(1)}, u32[]{:S(2)}, u32[]{:S(2)}) collective-permute-start(f32[3,3072]{1,0:T(4,128)S(1)} %get-tuple-element.435), channel_id=1, source_target_pairs={{16,0},{32,16},{48,32},{64,48},{80,64},{96,80},{112,96},{128,112},... | collective-permute-start | bytes 110600 | tf_op jit(solution)/shard_map/ppermute | solution.py:23
  46.6 22.5 %collective-permute-start = (f32[24]{0:T(128)S(1)}, f32[24]{0:T(128)S(1)}, u32[]{:S(2)}, u32[]{:S(2)}) collective-permute-start(f32[24]{0:T(128)S(1)} %get-tuple-element.439), channel_id=1, source_target_pairs={{16,0},{32,16},{48,32},{64,48},{80,64},{96,80},{112,96},{128,112},... | collective-permute-start | bytes 296 | tf_op jit(solution)/shard_map/ppermute | solution.py:23
  48.6 20.6 %collective-permute-start.1 = (f32[24]{0:T(128)S(1)}, f32[24]{0:T(128)S(1)}, u32[]{:S(2)}, u32[]{:S(2)}) collective-permute-start(f32[24]{0:T(128)S(1)} %get-tuple-element.440), channel_id=1, source_target_pairs={{0,16},{16,32},{32,48},{48,64},{64,80},{80,96},{96,112},{112,128},... | collective-permute-start | bytes 296 | tf_op jit(solution)/shard_map/ppermute | solution.py:23
  209.2 4.4 collective-permute-start.4
  211.1 5.9 collective-permute-start.5
  259.1 123.3 %collective-permute-start.7 = (f32[3,3072]{1,0:T(4,128)S(1)}, f32[3,3072]{1,0:T(4,128)S(1)}, u32[]{:S(2)}, u32[]{:S(2)}) collective-permute-start(f32[3,3072]{1,0:T(4,128)S(1)} %get-tuple-element.434), channel_id=1, source_target_pairs={{0,16},{16,32},{32,48},{48,64},{64,80},{80,96},{96,112},{112,128},... | collective-permute-start | bytes 110600 | tf_op jit(solution)/shard_map/ppermute | solution.py:23
  267.7 114.6 %collective-permute-start.6 = (f32[3,3072]{1,0:T(4,128)S(1)}, f32[3,3072]{1,0:T(4,128)S(1)}, u32[]{:S(2)}, u32[]{:S(2)}) collective-permute-start(f32[3,3072]{1,0:T(4,128)S(1)} %get-tuple-element.433), channel_id=1, source_target_pairs={{16,0},{32,16},{48,32},{64,48},{80,64},{96,80},{112,96},{128,112},... | collective-permute-start | bytes 110600 | tf_op jit(solution)/shard_map/ppermute | solution.py:23
  523.1 4.4 collective-permute-start.8
  525.4 5.9 collective-permute-start.9
where the time goes:
time: 672 us; the launch traced here: 665 us
  blocking collectives  257 us (38%)
  local copies, waits for them, and re-layouts  171 us (25%)
  matrix products  70.6 us (11%)
  other arithmetic  60.7 us (9%)
  loops' own time  59.3 us (9%)
  starting transfers between devices  34.8 us (5%)
  waiting for transfers between devices  7.42 us (1%)
    psum x2, blocking collectives, on_device(): energy_sum, share_sum = lax.psum((energy_part, share_part), ('line', 'seg'))  214 us
    gather x288, local copies, waits for them, and re-layouts  118 us
    psum x2, blocking collectives, on_device(): gram_sum, cross_sum = lax.psum((gram_matrix, cross_matrix), 'seg')  43.1 us
    another operation x24, loops' own time, one_turn(): return lax.cond(jnp.any(turn_cells >= 0), compute, skipped, 0)  43.1 us
    ppermute x10, starting transfers between devices, from_behind(): lax.ppermute(value, axis, [(source, source + steps) for source in range(i...  34.8 us
    dot_general x24, matrix products, match_block(): lax.dot_general(target, posterior, (((1,), (1,)), ((), ())), precision=la...  33.6 us
    dot_general x2, matrix products, on_device(): jnp.dot(linear_part, own_points, precision=lax.Precision.HIGHEST, preferr...  33.5 us
    gather x2, local copies, waits for them, and re-layouts, on_device(): jnp.take(own_points, safe_rows.reshape(-1), axis=1)  23 us
  transfers between devices with their start and end apart: 10, of which 2 were waited for; matrix products, arithmetic and copies ran while one was open for 3% of the time, Pallas kernels for 0%

commit v1 on v0

v1 whole, which is shorter than its diff:
```python
import functools
import math

import jax
import jax.numpy as jnp
from jax import lax
from jax.experimental import pallas as pl
from jax.experimental.pallas import tpu as pltpu
from jax.sharding import PartitionSpec as P

NCELL = 16
CT = 512
BLOCK = 128
ITERS = 2
SPREAD_START = 0.05
PRIOR_TOP = 0.05
LOG2E = math.log2(math.e)
MARGIN = NCELL * CT
CHUNK = 16
MESH = pl.DeviceIdType.MESH
F32 = jnp.float32


def iota(shape, dim):
    return lax.broadcasted_iota(jnp.int32, shape, dim)


def fetch_kernel(lines, segs, points, rows, pose, near, near_pose, src, own, table, own_sem, send_sem, recv_sem):
    me = lax.axis_index("line")
    upper, lower = lax.rem(me + 1, lines), lax.rem(me + lines - 1, lines)
    npts = points.shape[1]
    low_cols = pl.ds(0, MARGIN)
    high_cols = pl.ds(npts - MARGIN, MARGIN)

    barrier = pltpu.get_barrier_semaphore()
    for peer in (lower, upper):
        pl.semaphore_signal(barrier, inc=1, device_id={"line": peer}, device_id_type=MESH)
    locals_ = [
        pltpu.make_async_copy(points.at[:, cols], own.at[d], own_sem.at[d])
        for d, cols in enumerate((low_cols, high_cols))
    ]
    for copy in locals_:
        copy.start()
    pl.semaphore_wait(barrier, 2)

    def remote(source, target, slot, peer):
        return pltpu.make_async_remote_copy(
            src_ref=source,
            dst_ref=target,
            send_sem=send_sem.at[slot],
            recv_sem=recv_sem.at[slot],
            device_id={"line": peer},
            device_id_type=MESH,
        )

    sends = [
        remote(points.at[:, high_cols], near.at[0], 0, upper),
        remote(points.at[:, low_cols], near.at[1], 1, lower),
        remote(pose, near_pose.at[0], 2, upper),
        remote(pose, near_pose.at[1], 3, lower),
    ]
    for copy in sends:
        copy.start()

    table[...] = jnp.zeros_like(table)
    for copy in locals_:
        copy.wait()
    pairs = MARGIN // 256
    for d in range(2):
        for u in range(pairs):
            table[d, u, 0:3, :] = own[d, :, 256 * u : 256 * u + 128]
            table[d, u, 4:7, :] = own[d, :, 256 * u + 128 : 256 * u + 256]

    sub = iota((8, BLOCK), 0)
    shift = (sub >= 4).astype(jnp.int32)
    blocks = rows.shape[1] // BLOCK
    for d in range(2):

        @pl.loop(0, blocks)
        def _(b):
            index = rows[d : d + 1, pl.ds(pl.multiple_of(b * BLOCK, BLOCK), BLOCK)]
            live = index >= 0
            local = index if d == 0 else index - (npts - MARGIN)
            lane = jnp.broadcast_to(jnp.bitwise_and(local, 127), (8, BLOCK))
            high = jnp.broadcast_to(jnp.right_shift(local, 7), (8, BLOCK)) - shift
            total = jnp.zeros((8, BLOCK), F32)
            for u in range(pairs):
                taken = jnp.take_along_axis(table[d, u], lane, axis=1, mode="promise_in_bounds")
                total = jnp.where(high == 2 * u, taken, total)
            both = total + pltpu.roll(total, 4, 0)
            alive = jnp.broadcast_to(live.astype(F32), (8, BLOCK))
            tail = jnp.where(sub == 3, 1.0, jnp.where(sub == 4, alive, 0.0))
            src[d * blocks + b] = jnp.where(sub < 3, both, tail)

    for copy in sends:
        copy.wait()


def fetch(points, rows, pose, lines, segs):
    blocks = rows.shape[0] * rows.shape[1] // BLOCK
    vmem = pl.BlockSpec(memory_space=pltpu.VMEM)
    return pl.pallas_call(
        functools.partial(fetch_kernel, lines, segs),
        out_shape=(
            jax.ShapeDtypeStruct((2, 3, MARGIN), F32),
            jax.ShapeDtypeStruct((2, 12, 1), F32),
            jax.ShapeDtypeStruct((blocks, 8, BLOCK), F32),
        ),
        in_specs=[pl.BlockSpec(memory_space=pl.ANY), vmem, vmem],
        out_specs=(vmem, vmem, vmem),
        scratch_shapes=[
            pltpu.VMEM((2, 3, MARGIN), F32),
            pltpu.VMEM((2, MARGIN // 256, 8, 128), F32),
            pltpu.SemaphoreType.DMA((2,)),
            pltpu.SemaphoreType.DMA((4,)),
            pltpu.SemaphoreType.DMA((4,)),
        ],
        compiler_params=pltpu.CompilerParams(collective_id=0, has_side_effects=True),
        name="fetch",
    )(points, rows, pose)


def pose_columns(column):
    wide = jnp.broadcast_to(column, (12, BLOCK))
    sub = iota((8, BLOCK), 0)
    zero = jnp.zeros((8, BLOCK), F32)
    columns = []
    for c in range(4):
        value = jnp.where(sub == 3, 1.0, zero) if c == 3 else zero
        for k in range(3):
            row = 3 * k + c if c < 3 else 9 + k
            value = jnp.where(sub == k, jnp.broadcast_to(wide[row : row + 1], (8, BLOCK)), value)
        columns.append(value)
    return columns


def apply_pose(columns, tile):
    total = columns[3]
    for c in range(3):
        total = total + columns[c] * jnp.broadcast_to(tile[c : c + 1], (8, BLOCK))
    return total


def em_kernel(
    lines, segs, src, near, near_pose, pose, cells, matched, fitted, final_spread,
    targets, halves, weights, energies, row_out, line_out, seg_in, line_in,
    seg_send, seg_recv, line_send, line_recv,
):
    my_line, my_seg = lax.axis_index("line"), lax.axis_index("seg")
    blocks = src.shape[0] // 2
    tiles = CT // BLOCK
    sub = iota((8, BLOCK), 0)
    lanes = iota((8, BLOCK), 1)

    barrier = pltpu.get_barrier_semaphore()

    @pl.loop(1, segs)
    def _(k):
        pl.semaphore_signal(
            barrier, inc=1, device_id={"seg": lax.rem(my_seg + k, segs)}, device_id_type=MESH
        )

    @pl.loop(1, lines)
    def _(k):
        pl.semaphore_signal(
            barrier, inc=1, device_id={"line": lax.rem(my_line + k, lines)}, device_id_type=MESH
        )

    def seg_copy(it, k):
        return pltpu.make_async_remote_copy(
            src_ref=row_out.at[it],
            dst_ref=seg_in.at[it, my_seg],
            send_sem=seg_send.at[it, k],
            recv_sem=seg_recv.at[it, my_seg],
            device_id={"seg": lax.rem(my_seg + k, segs)},
            device_id_type=MESH,
        )

    def line_copy(it, k):
        return pltpu.make_async_remote_copy(
            src_ref=line_out.at[it],
            dst_ref=line_in.at[it, my_line],
            send_sem=line_send.at[it, k],
            recv_sem=line_recv.at[it, my_line],
            device_id={"line": lax.rem(my_line + k, lines)},
            device_id_type=MESH,
        )

    def seg_arrival(it, k):
        other = lax.rem(my_seg + k, segs)
        return pltpu.make_async_remote_copy(
            src_ref=row_out.at[it],
            dst_ref=seg_in.at[it, other],
            send_sem=seg_send.at[it, k],
            recv_sem=seg_recv.at[it, other],
            device_id={"seg": other},
            device_id_type=MESH,
        )

    def line_arrival(it, k):
        other = lax.rem(my_line + k, lines)
        return pltpu.make_async_remote_copy(
            src_ref=line_out.at[it],
            dst_ref=line_in.at[it, other],
            send_sem=line_send.at[it, k],
            recv_sem=line_recv.at[it, other],
            device_id={"line": other},
            device_id_type=MESH,
        )

    own_pose = pose_columns(pose[...])
    low_pose = pose_columns(near_pose[0])
    up_pose = pose_columns(near_pose[1])
    spread = jnp.full((8, BLOCK), SPREAD_START, F32)

    for it in range(ITERS):
        last = it == ITERS - 1
        square = LOG2E / (2.0 * spread)
        scale = jnp.sqrt(square)
        back = 1.0 / scale
        back_square = 2.0 * spread / LOG2E
        rows_scale = jnp.where(sub < 3, scale, 1.0)
        own_scaled = [column * rows_scale for column in own_pose]
        near_scaled = [
            [column * rows_scale for column in low_pose],
            [column * rows_scale for column in up_pose],
        ]
        row_back = jnp.where(sub < 3, back, jnp.where(sub == 4, back_square, 1.0))

        for d in range(2):

            @pl.loop(0, NCELL)
            def _(c):
                for t in range(tiles):
                    start = pl.multiple_of(c * CT + t * BLOCK, BLOCK)
                    tile = near[d, :, pl.ds(start, BLOCK)]
                    value = apply_pose(near_scaled[d], tile)
                    here = slice(t * BLOCK, (t + 1) * BLOCK)
                    targets[d * NCELL + c, :, here] = value
                    first = value.astype(jnp.bfloat16).astype(F32)
                    rest = value - first
                    second = rest.astype(jnp.bfloat16).astype(F32)
                    third = rest - second
                    packed = jnp.concatenate([first, second, third, jnp.zeros_like(first)], axis=0)
                    halves[d * NCELL + c, :, here] = packed.astype(jnp.bfloat16)

        sums = [jnp.zeros((8, BLOCK), F32) for _ in range(7)]
        for d in range(2):

            def one_block(b, sums):
                x = src[d * blocks + b]
                cell = jnp.maximum(cells[d, b], 0) + d * NCELL
                moved = jnp.transpose(apply_pose(own_scaled, x))
                y = [targets[cell, k : k + 1, :] for k in range(3)]
                for i in range(BLOCK // CHUNK):
                    here = slice(i * CHUNK, (i + 1) * CHUNK)
                    distance = None
                    for k in range(3):
                        gap = moved[here, k : k + 1] - y[k]
                        distance = gap * gap if distance is None else distance + gap * gap
                    weight = lax.exp2(-distance)
                    part = weight * distance
                    energy = part[:, :BLOCK]
                    for t in range(1, tiles):
                        energy = energy + part[:, t * BLOCK : (t + 1) * BLOCK]
                    energies[here, :] = energy
                    high = weight.astype(jnp.bfloat16)
                    weights[here, :] = high
                    weights[BLOCK + i * CHUNK : BLOCK + (i + 1) * CHUNK, :] = (
                        weight - high.astype(F32)
                    ).astype(jnp.bfloat16)
                out = lax.dot_general(
                    halves[cell],
                    weights[...],
                    (((1,), (1,)), ((), ())),
                    preferred_element_type=F32,
                )
                out = out[:, :BLOCK] + out[:, BLOCK:]
                pulled = out[0:8] + (out[8:16] + jnp.where(sub == 3, 0.0, out[16:24]))
                energy = jnp.sum(jnp.transpose(energies[...]), axis=0, keepdims=True)
                total = pulled[3:4]
                factor = x[4:5] / (total + 1.0)
                merged = jnp.where(sub == 4, jnp.broadcast_to(energy, (8, BLOCK)), pulled)
                result = merged * row_back * jnp.broadcast_to(factor, (8, BLOCK))
                if last:
                    matched[d, :, pl.ds(pl.multiple_of(b * BLOCK, BLOCK), BLOCK)] = result[0:5]
                share = jnp.broadcast_to(result[3:4], (8, BLOCK))
                weighted = share * x
                new = []
                for c in range(4):
                    new.append(sums[c] + (result * jnp.broadcast_to(x[c : c + 1], (8, BLOCK)) if c < 3 else result))
                for c in range(3):
                    new.append(sums[4 + c] + weighted * jnp.broadcast_to(x[c : c + 1], (8, BLOCK)))
                return tuple(new)

            sums = lax.fori_loop(0, blocks, one_block, tuple(sums))

        row = jnp.zeros((8, BLOCK), F32)
        for q in range(7):
            column = jnp.sum(sums[q], axis=1, keepdims=True)
            row = row + jnp.where(lanes == 8 * q + sub, jnp.broadcast_to(column, (8, BLOCK)), 0.0)
        row = jnp.sum(row, axis=0, keepdims=True)
        row_out[it] = row
        seg_in[it, my_seg] = row
        if it == 0:
            pl.semaphore_wait(barrier, segs + lines - 2)

        @pl.loop(1, segs)
        def _(k):
            seg_copy(it, k).start()

        kept = jnp.zeros((8, BLOCK), F32)
        for c in range(4):
            kept = kept + jnp.where((lanes == 64 + 8 * c + sub) & (sub < 3), own_pose[c], 0.0)
        kept = jnp.sum(kept, axis=0, keepdims=True)

        @pl.loop(1, segs)
        def _(k):
            seg_arrival(it, k).wait_recv()

        line_row = kept + jnp.sum(seg_in[it], axis=0)
        line_out[it] = line_row
        line_in[it, my_line] = line_row

        @pl.loop(1, lines)
        def _(k):
            line_copy(it, k).start()

        @pl.loop(1, lines)
        def _(k):
            line_arrival(it, k).wait_recv()

        whole = line_in[it].reshape(lines, BLOCK)
        turned = jnp.transpose(jnp.concatenate([whole, jnp.zeros((BLOCK - lines, BLOCK), F32)], axis=0))
        part = [turned[8 * q : 8 * q + 8] for q in range(12)]

        def entry(q, r):
            return jnp.broadcast_to(part[q][r : r + 1], (8, BLOCK))

        n = [[None] * 4 for _ in range(4)]
        for a in range(3):
            for c in range(a + 1):
                n[a][c] = entry(4 + c, a)
        for c in range(4):
            n[3][c] = entry(c, 3)
        share_sum = jnp.sum(n[3][3], axis=1, keepdims=True)
        energy_sum = jnp.sum(entry(3, 4), axis=1, keepdims=True)
        spread = jnp.broadcast_to((energy_sum + PRIOR_TOP) / (3.0 * share_sum + 1.0), (8, BLOCK))
        for a in range(4):
            n[a][a] = n[a][a] + 1.0
        low = [[None] * 4 for _ in range(4)]
        inverse = [None] * 4
        for c in range(4):
            diagonal = n[c][c]
            for j in range(c):
                diagonal = diagonal - low[c][j] * n[c][j]
            inverse[c] = 1.0 / diagonal
            for a in range(c + 1, 4):
                for j in range(c):
                    n[a][c] = n[a][c] - low[c][j] * n[a][j]
                low[a][c] = n[a][c] * inverse[c]
        z = [part[c] + part[8 + c] for c in range(4)]
        for a in range(4):
            for c in range(a):
                z[a] = z[a] - low[a][c] * z[c]
        z = [z[a] * inverse[a] for a in range(4)]
        for a in range(3, -1, -1):
            for c in range(a + 1, 4):
                z[a] = z[a] - low[c][a] * z[c]

        def pick(which):
            columns = []
            for c in range(4):
                value = jnp.sum(jnp.where((lanes == which) & (sub < 3), z[c], 0.0), axis=1, keepdims=True)
                value = jnp.broadcast_to(value, (8, BLOCK))
                columns.append(jnp.where(sub == 3, 1.0, value) if c == 3 else value)
            return columns

        own_pose = pick(my_line)
        if not last:
            low_pose = pick(my_line - 1)
            up_pose = pick(my_line + 1)

    for k in range(3):
        for c in range(3):
            fitted[3 * k + c : 3 * k + c + 1, :] = own_pose[c][k : k + 1, 0:1]
        fitted[9 + k : 10 + k, :] = own_pose[3][k : k + 1, 0:1]
    final_spread[...] = spread[0:1, 0:1]

    for it in range(ITERS):

        @pl.loop(1, segs)
        def _(k):
            seg_copy(it, k).wait_send()

        @pl.loop(1, lines)
        def _(k):
            line_copy(it, k).wait_send()


def em(src, near, near_pose, pose, cells, lines, segs):
    blocks = src.shape[0]
    vmem = pl.BlockSpec(memory_space=pltpu.VMEM)
    smem = pl.BlockSpec(memory_space=pltpu.SMEM)
    return pl.pallas_call(
        functools.partial(em_kernel, lines, segs),
        out_shape=(
            jax.ShapeDtypeStruct((2, 5, blocks // 2 * BLOCK), F32),
            jax.ShapeDtypeStruct((12, 1), F32),
            jax.ShapeDtypeStruct((1, 1), F32),
        ),
        in_specs=[vmem, vmem, vmem, vmem, smem],
        out_specs=(vmem, vmem, vmem),
        scratch_shapes=[
            pltpu.VMEM((2 * NCELL, 8, CT), F32),
            pltpu.VMEM((2 * NCELL, 32, CT), jnp.bfloat16),
            pltpu.VMEM((2 * BLOCK, CT), jnp.bfloat16),
            pltpu.VMEM((BLOCK, BLOCK), F32),
            pltpu.VMEM((ITERS, 1, BLOCK), F32),
            pltpu.VMEM((ITERS, 1, BLOCK), F32),
            pltpu.VMEM((ITERS, segs, 1, BLOCK), F32),
            pltpu.VMEM((ITERS, lines, 1, BLOCK), F32),
            pltpu.SemaphoreType.DMA((ITERS, segs)),
            pltpu.SemaphoreType.DMA((ITERS, segs)),
            pltpu.SemaphoreType.DMA((ITERS, lines)),
            pltpu.SemaphoreType.DMA((ITERS, lines)),
        ],
        compiler_params=pltpu.CompilerParams(collective_id=1, has_side_effects=True),
        name="em",
    )(src, near, near_pose, pose, cells)


def solution(mesh):
    lines, segs = mesh.shape["line"], mesh.shape["seg"]

    def on_device(points, rows, cells, pose):
        near, near_pose, src = fetch(points[0, 0], rows[0, 0], pose, lines, segs)
        matched, fitted, spread = em(src, near, near_pose, pose, cells[0, 0], lines, segs)
        return matched[None, None], fitted, spread.reshape(1)

    return jax.shard_map(
        on_device,
        mesh=mesh,
        in_specs=(
            P("line", "seg", None, None),
            P("line", "seg", None, None),
            P("line", "seg", None, None),
            P(None, "line"),
        ),
        out_specs=(P("line", "seg", None, None, None), P(None, "line"), P()),
        check_vma=False,
    )
```

time: 672 us -> 101 us (0.15); the launches traced: 665 us -> 101 us
  blocking collectives: 257 us -> 0 us
  local copies, waits for them, and re-layouts: 171 us -> 5.66 us
  Pallas kernels: 0 us -> 92.7 us
  matrix products: 70.6 us -> 0 us
  other arithmetic: 60.7 us -> 0 us
  loops' own time: 59.3 us -> 0 us
  starting transfers between devices: 34.8 us -> 0 us
  waiting for transfers between devices: 7.42 us -> 0 us
    psum x4 -> x0, blocking collectives: 257 us -> none  [the longest x2 214 us: on_device(): energy_sum, share_sum = lax.psum((energy_part, share_part), ('line', 'seg'))]
    gather x290 -> x0, local copies, waits for them, and re-layouts: 141 us -> none
    pallas_call x0 -> x2, Pallas kernels: none -> 92.7 us  [the longest x1 78.1 us: em(): pl.pallas_call(functools.partial(em_kernel, lines, segs), out_shape=(jax....]
    dot_general x32 -> x0, matrix products: 69.8 us -> none  [the longest x24 33.6 us: match_block(): lax.dot_general(target, posterior, (((1,), (1,)), ((), ())), precision=la...]
    another operation x50 -> x0, loops' own time: 59.3 us -> none  [the longest x24 43.1 us: one_turn(): return lax.cond(jnp.any(turn_cells >= 0), compute, skipped, 0)]
    ppermute x10 -> x0, starting transfers between devices: 34.8 us -> none  [from_behind(): lax.ppermute(value, axis, [(source, source + steps) for source in range(i...]
    reduce_sum x50 -> x0, other arithmetic: 34.1 us -> none  [the longest x24 18 us: match_block(): energy_row = jnp.sum(posterior * distance, axis=1)]
    reduce_or x24 -> x0, other arithmetic: 15.3 us -> none  [one_turn(): return lax.cond(jnp.any(turn_cells >= 0), compute, skipped, 0)]
  transfers between devices with their start and end apart: 10 -> 0, of which waited for: 2 -> 0; matrix products, arithmetic and copies ran while one was open for 3% -> 0% of each run, Pallas kernels for 0% -> 0%
where the time goes in v1:
time: 101 us
  Pallas kernels  92.7 us (92%)
  local copies, waits for them, and re-layouts  5.66 us (6%)
  between operations  2.43 us (2%)
    pallas_call x1, Pallas kernels, em(): pl.pallas_call(functools.partial(em_kernel, lines, segs), out_shape=(jax....  78.1 us
    pallas_call x1, Pallas kernels, fetch(): pl.pallas_call(functools.partial(fetch_kernel, lines, segs), out_shape=(j...  14.6 us
    unnamed x8, local copies, waits for them, and re-layouts  5.66 us

profile of v1, /device:TPU:1, one launch (start us, length us, event | category | flops | bytes accessed | tf_op | source)
XLA Modules:
  0.0 100.8 jit_solution(17443421477955425774)
XLA Ops:
  0.6 0.0 copy-start.1
  0.6 0.6 copy-done.1
  1.3 0.7 copy.7.pose
  2.0 2.1 %copy.13 = f32[1,1,3,32768]{3,2,1,0:T(4,128)} copy(f32[1,1,3,32768]{3,1,2,0:T(1,128)} %param.4) | data formatting | bytes 786432
  4.0 14.6 %fetch.1 = (f32[2,3,8192]{2,1,0:T(4,128)}, f32[2,12,1]{2,1,0:T(8,128)}, f32[48,8,128]{2,1,0:T(8,128)}) custom-call(f32[3,32768]{1,0:T(4,128)} %bitcast.7, s32[2,3072]{1,0:T(2,128)} %bitcast.9, f32[12,1]{1,0:T(8,128)} %copy.7.pose), custom_call_target="tpu_custom_call" | custom-call | tf_op jit(solution)/shard_map/fetch/pallas_call | solution.py:102
  18.6 78.1 %em.1 = (f32[2,5,3072]{2,1,0:T(8,128)}, f32[12,1]{1,0:T(8,128)}, f32[1,1]{1,0:T(1,128)}) custom-call(f32[48,8,128]{2,1,0:T(8,128)} %get-tuple-element.9.src, f32[2,3,8192]{2,1,0:T(4,128)} %get-tuple-element.10.near, f32[2,12,1]{2,1,0:T(8,128)} %get-tuple-element.11.near_pose, f32[12,1]{1,0:T(8,128)} %copy.7.pose, s32[2,24]{1,0:T(2,128)} %bitcast.10), custom_call_target="tpu_custom_call" | custom-call | tf_op jit(solution)/shard_map/em/pallas_call | solution.py:405
  96.8 0.0 copy-start
  96.8 1.7 %copy.9 = f32[1,1,2,5,3072]{4,2,3,1,0:T(2,128)} copy(f32[1,1,2,5,3072]{4,3,2,1,0:T(8,128)} %bitcast.8) | data formatting | bytes 245760
  98.5 0.0 copy-done
  98.5 0.6 copy.10
Async XLA Ops:
  0.6 0.7 copy-start.1
  96.8 1.7 %copy-start = (f32[12,1]{1,0:T(8,128)S(1)}, f32[12,1]{1,0:T(8,128)}, u32[]{:S(2)}) copy-start(f32[12,1]{1,0:T(8,128)} %get-tuple-element.16) | copy-start | bytes 148

commit v2 on v1

v2 whole, which is shorter than its diff:
```python
import functools
import math

import jax
import jax.numpy as jnp
from jax import lax
from jax.experimental import pallas as pl
from jax.experimental.pallas import tpu as pltpu
from jax.sharding import PartitionSpec as P

NCELL = 16
CT = 512
BLOCK = 128
ITERS = 2
SPREAD_START = 0.05
PRIOR_TOP = 0.05
LOG2E = math.log2(math.e)
MARGIN = NCELL * CT
CHUNK = 16
UNROLL = 8
GATHER = 4
VMEM_LIMIT = 16 << 20
MESH = pl.DeviceIdType.MESH
F32 = jnp.float32


def iota(shape, dim):
    return lax.broadcasted_iota(jnp.int32, shape, dim)


def fetch_kernel(lines, points, rows, pose, near, near_pose, src, own, own_sem, send_sem, recv_sem):
    me = lax.axis_index("line")
    upper, lower = lax.rem(me + 1, lines), lax.rem(me + lines - 1, lines)
    tiles = points.shape[1]
    margin_tiles = MARGIN // BLOCK
    low_tiles = pl.ds(0, margin_tiles)
    high_tiles = pl.ds(tiles - margin_tiles, margin_tiles)

    barrier = pltpu.get_barrier_semaphore()
    for peer in (lower, upper):
        pl.semaphore_signal(barrier, inc=1, device_id={"line": peer}, device_id_type=MESH)
    locals_ = [
        pltpu.make_async_copy(points.at[:, part], own.at[d], own_sem.at[d])
        for d, part in enumerate((low_tiles, high_tiles))
    ]
    for copy in locals_:
        copy.start()

    def remote(source, target, slot, peer):
        return pltpu.make_async_remote_copy(
            src_ref=source,
            dst_ref=target,
            send_sem=send_sem.at[slot],
            recv_sem=recv_sem.at[slot],
            device_id={"line": peer},
            device_id_type=MESH,
        )

    sends = [
        remote(points.at[:, high_tiles], near.at[0], 0, upper),
        remote(points.at[:, low_tiles], near.at[1], 1, lower),
        remote(pose, near_pose.at[0], 2, upper),
        remote(pose, near_pose.at[1], 3, lower),
    ]
    sub = iota((8, BLOCK), 0)
    blocks = rows.shape[1] // BLOCK

    def gather(d):
        @pl.loop(0, blocks // GATHER)
        def _(turn):
            for g in range(GATHER):
                b = turn * GATHER + g
                index = rows[d : d + 1, pl.ds(pl.multiple_of(b * BLOCK, BLOCK), BLOCK)]
                live = index >= 0
                local = index if d == 0 else index - (tiles * BLOCK - MARGIN)
                lane = jnp.broadcast_to(jnp.bitwise_and(local, 127), (8, BLOCK))
                high = jnp.broadcast_to(jnp.right_shift(local, 7), (8, BLOCK)) - sub
                found = [jnp.zeros((8, BLOCK), F32) for _ in range(3)]
                for u in range(margin_tiles // 8):
                    here = high == 8 * u
                    for k in range(3):
                        taken = jnp.take_along_axis(
                            own[d, k, 8 * u : 8 * u + 8, :], lane, axis=1, mode="promise_in_bounds"
                        )
                        found[k] = jnp.where(here, taken, found[k])
                alive = jnp.broadcast_to(live.astype(F32), (8, BLOCK))
                value = jnp.where(sub == 3, 1.0, jnp.where(sub == 4, alive, 0.0))
                for k in range(3):
                    picked = jnp.sum(found[k], axis=0, keepdims=True)
                    value = jnp.where(sub == k, jnp.broadcast_to(picked, (8, BLOCK)), value)
                src[d * blocks + b] = value

    pl.semaphore_wait(barrier, 2)
    for copy in sends:
        copy.start()
    for d in range(2):
        locals_[d].wait()
        gather(d)
    for copy in sends:
        copy.wait()


def fetch(points, rows, pose, lines):
    blocks = rows.shape[0] * rows.shape[1] // BLOCK
    vmem = pl.BlockSpec(memory_space=pltpu.VMEM)
    return pl.pallas_call(
        functools.partial(fetch_kernel, lines),
        out_shape=(
            jax.ShapeDtypeStruct((2, 3, MARGIN // BLOCK, BLOCK), F32),
            jax.ShapeDtypeStruct((2, 1, 12), F32),
            jax.ShapeDtypeStruct((blocks, 8, BLOCK), F32),
        ),
        in_specs=[pl.BlockSpec(memory_space=pl.ANY), vmem, vmem],
        out_specs=(vmem, vmem, vmem),
        scratch_shapes=[
            pltpu.VMEM((2, 3, MARGIN // BLOCK, BLOCK), F32),
            pltpu.SemaphoreType.DMA((2,)),
            pltpu.SemaphoreType.DMA((4,)),
            pltpu.SemaphoreType.DMA((4,)),
        ],
        compiler_params=pltpu.CompilerParams(
            collective_id=0, has_side_effects=True, vmem_limit_bytes=VMEM_LIMIT
        ),
        name="fetch",
    )(points, rows, pose)


def pose_columns(row):
    sub = iota((8, BLOCK), 0)
    columns = []
    for c in range(4):
        value = jnp.zeros((8, BLOCK), F32)
        for k in range(3):
            lane = 3 * k + c if c < 3 else 9 + k
            value = jnp.where(sub == k, jnp.broadcast_to(row[:, lane : lane + 1], (8, BLOCK)), value)
        columns.append(value)
    return columns


def apply_pose(columns, coordinates):
    total = columns[3]
    for c in range(3):
        total = total + columns[c] * jnp.broadcast_to(coordinates[c], (8, BLOCK))
    return total


def split3(value):
    first = value.astype(jnp.bfloat16).astype(F32)
    rest = value - first
    second = rest.astype(jnp.bfloat16).astype(F32)
    return first, second, rest - second


def operand(value, norm_first):
    sub = iota((8, BLOCK), 0)
    norm = -jnp.sum(value * value, axis=0, keepdims=True)
    norms = [jnp.broadcast_to(part, (8, BLOCK)) for part in split3(norm)]
    if norm_first:
        value = 2.0 * value
        order = (0, 0, 0, 1, 1, 2, 1, 2)
        extra = norms + [1.0, 1.0, 1.0]
    else:
        order = (0, 1, 2, 0, 1, 0, 2, 1)
        extra = [1.0, 1.0, 1.0] + norms
    parts = split3(value)
    groups = [parts[p] for p in order]
    for i in range(6):
        groups[i] = jnp.where(sub == 3, extra[i], groups[i])
    return jnp.concatenate(groups, axis=0)


def em_kernel(
    lines, segs, src, near, near_pose, pose, cells, matched, fitted, final_spread,
    side_y, side_m, centres, weights, energies, row_out, line_out, seg_in, line_in,
    seg_send, seg_recv, line_send, near_recv, line_recv,
):
    my_line, my_seg = lax.axis_index("line"), lax.axis_index("seg")
    blocks = src.shape[0] // 2
    tiles = CT // BLOCK
    sub = iota((8, BLOCK), 0)
    lanes = iota((8, BLOCK), 1)

    barrier = pltpu.get_barrier_semaphore()

    @pl.loop(1, segs)
    def _(k):
        pl.semaphore_signal(
            barrier, inc=1, device_id={"seg": lax.rem(my_seg + k, segs)}, device_id_type=MESH
        )

    @pl.loop(1, lines)
    def _(k):
        pl.semaphore_signal(
            barrier, inc=1, device_id={"line": lax.rem(my_line + k, lines)}, device_id_type=MESH
        )

    seg_order = sorted(range(1, segs), key=lambda k: -min(k, segs - k))
    line_order = [1, lines - 1] + sorted(range(2, lines - 1), key=lambda k: -min(k, lines - k))

    def seg_copy(it, k):
        return pltpu.make_async_remote_copy(
            src_ref=row_out.at[it],
            dst_ref=seg_in.at[it, my_seg],
            send_sem=seg_send.at[it],
            recv_sem=seg_recv.at[it],
            device_id={"seg": lax.rem(my_seg + k, segs)},
            device_id_type=MESH,
        )

    def line_copy(it, k):
        arrived = line_recv.at[it]
        if k == 1:
            arrived = near_recv.at[it, 0]
        elif k == lines - 1:
            arrived = near_recv.at[it, 1]
        return pltpu.make_async_remote_copy(
            src_ref=line_out.at[it],
            dst_ref=line_in.at[it, my_line],
            send_sem=line_send.at[it],
            recv_sem=arrived,
            device_id={"line": lax.rem(my_line + k, lines)},
            device_id_type=MESH,
        )

    def wait_rows(buffer, count, sem):
        part = buffer.at[pl.ds(0, count)]
        pltpu.make_async_copy(part, part, sem).wait()

    lower, upper = lax.rem(my_line + lines - 1, lines), lax.rem(my_line + 1, lines)

    own_pose = pose_columns(pose[...])
    low_pose = pose_columns(near_pose[0])
    up_pose = pose_columns(near_pose[1])
    spread = jnp.full((8, BLOCK), SPREAD_START, F32)

    def prepare(own_pose, low_pose, up_pose):
        for d in range(2):

            @pl.loop(0, NCELL)
            def _(c):
                world = []
                for t in range(tiles):
                    raw = [near[d, k, pl.ds(c * tiles + t, 1), :] for k in range(3)]
                    world.append(apply_pose((low_pose, up_pose)[d], raw))
                centre = world[0]
                for t in range(1, tiles):
                    centre = centre + world[t]
                centre = jnp.sum(centre, axis=1, keepdims=True) * (1.0 / CT)
                centre = jnp.broadcast_to(centre, (8, BLOCK))
                centres[d * NCELL + c] = centre
                for t in range(tiles):
                    here = slice(t * BLOCK, (t + 1) * BLOCK)
                    value = operand(world[t] - centre, False)
                    side_y[d * NCELL + c, :, here] = value.astype(jnp.bfloat16)

        for d in range(2):

            @pl.loop(0, blocks // UNROLL)
            def _(turn):
                for u in range(UNROLL):
                    b = turn * UNROLL + u
                    x = src[d * blocks + b]
                    cell = jnp.maximum(cells[d, b], 0) + d * NCELL
                    moved = apply_pose(own_pose, [x[k : k + 1] for k in range(3)])
                    value = operand(moved - centres[cell], True)
                    side_m[d * blocks + b] = jnp.transpose(value).astype(jnp.bfloat16)

    prepare(own_pose, low_pose, up_pose)
    for it in range(ITERS):
        last = it == ITERS - 1
        rate = LOG2E / (2.0 * spread)
        rate = jnp.concatenate([rate] * (CHUNK // 8), axis=0)
        rate = jnp.concatenate([rate] * tiles, axis=1)

        sums = [jnp.zeros((8, BLOCK), F32) for _ in range(7)]
        for d in range(2):

            def one_block(b, u, sums):
                x = src[d * blocks + b]
                cell = jnp.maximum(cells[d, b], 0) + d * NCELL
                exponents = jnp.dot(side_m[d * blocks + b], side_y[cell], preferred_element_type=F32)
                for i in range(BLOCK // CHUNK):
                    here = slice(i * CHUNK, (i + 1) * CHUNK)
                    exponent = exponents[here]
                    weight = lax.exp2(exponent * rate)
                    part = weight * exponent
                    energy = part[:, :BLOCK]
                    for t in range(1, tiles):
                        energy = energy + part[:, t * BLOCK : (t + 1) * BLOCK]
                    energies[u, here, :] = energy
                    high = weight.astype(jnp.bfloat16)
                    weights[u, here, 0:CT] = high
                    weights[u, here, CT : 2 * CT] = (weight - high.astype(F32)).astype(jnp.bfloat16)
                values = side_y[cell, 0:32, :]
                out = lax.dot_general(
                    weights[u],
                    jnp.concatenate([values, values], axis=1),
                    (((1,), (1,)), ((), ())),
                    preferred_element_type=F32,
                )
                out = jnp.transpose(out)
                pulled = out[0:8] + jnp.where(sub == 3, 0.0, out[8:16] + out[16:24])
                energy = jnp.sum(jnp.transpose(energies[u]), axis=0, keepdims=True)
                total = jnp.broadcast_to(pulled[3:4], (8, BLOCK))
                factor = jnp.broadcast_to(x[4:5], (8, BLOCK)) / (total + 1.0)
                merged = jnp.where(sub == 4, jnp.broadcast_to(-energy, (8, BLOCK)), pulled)
                result = (merged + centres[cell] * total) * factor
                if last:
                    here = pl.ds(pl.multiple_of(b * BLOCK, BLOCK), BLOCK)
                    for k in range(5):
                        matched[k, d : d + 1, here] = result[k : k + 1]
                share = jnp.broadcast_to(result[3:4], (8, BLOCK))
                weighted = share * x
                new = []
                for c in range(4):
                    new.append(sums[c] + (result * jnp.broadcast_to(x[c : c + 1], (8, BLOCK)) if c < 3 else result))
                for c in range(3):
                    new.append(sums[4 + c] + weighted * jnp.broadcast_to(x[c : c + 1], (8, BLOCK)))
                return tuple(new)

            def some_blocks(turn, sums):
                for u in range(UNROLL):
                    sums = one_block(turn * UNROLL + u, u, sums)
                return sums

            sums = lax.fori_loop(0, blocks // UNROLL, some_blocks, tuple(sums))

        row = jnp.zeros((8, BLOCK), F32)
        for q in range(7):
            column = jnp.sum(sums[q], axis=1, keepdims=True)
            row = row + jnp.where(lanes == 8 * q + sub, jnp.broadcast_to(column, (8, BLOCK)), 0.0)
        row = jnp.sum(row, axis=0, keepdims=True)
        row_out[it] = row
        seg_in[it, my_seg] = row
        if it == 0:
            pl.semaphore_wait(barrier, segs + lines - 2)
        for k in seg_order:
            seg_copy(it, k).start()

        kept = jnp.zeros((8, BLOCK), F32)
        for c in range(4):
            kept = kept + jnp.where((lanes == 64 + 8 * c + sub) & (sub < 3), own_pose[c], 0.0)
        kept = jnp.sum(kept, axis=0, keepdims=True)

        wait_rows(seg_in.at[it], segs - 1, seg_recv.at[it])
        line_row = kept + jnp.sum(seg_in[it], axis=0)
        line_out[it] = line_row
        line_in[it, my_line] = line_row
        for k in line_order:
            line_copy(it, k).start()
        wait_rows(seg_in.at[it], segs - 1, seg_send.at[it])
        for k in range(2):
            wait_rows(line_in.at[it], 1, near_recv.at[it, k])

        three = jnp.where(sub == 0, line_in[it, lower], jnp.where(sub == 1, line_row, line_in[it, upper]))
        turned = jnp.transpose(three)
        part = [jnp.concatenate([turned[8 * q : 8 * q + 8], jnp.zeros((8, BLOCK - 8), F32)], axis=1) for q in range(12)]

        def entry(q, r):
            return jnp.broadcast_to(part[q][r : r + 1], (8, BLOCK))

        n = [[None] * 4 for _ in range(4)]
        for a in range(3):
            for c in range(a + 1):
                n[a][c] = entry(4 + c, a)
        for c in range(4):
            n[3][c] = entry(c, 3)
        for a in range(4):
            n[a][a] = n[a][a] + 1.0
        low = [[None] * 4 for _ in range(4)]
        inverse = [None] * 4
        for c in range(4):
            diagonal = n[c][c]
            for j in range(c):
                diagonal = diagonal - low[c][j] * n[c][j]
            inverse[c] = 1.0 / diagonal
            for a in range(c + 1, 4):
                for j in range(c):
                    n[a][c] = n[a][c] - low[c][j] * n[a][j]
                low[a][c] = n[a][c] * inverse[c]
        z = [part[c] + part[8 + c] for c in range(4)]
        for a in range(4):
            for c in range(a):
                z[a] = z[a] - low[a][c] * z[c]
        z = [z[a] * inverse[a] for a in range(4)]
        for a in range(3, -1, -1):
            for c in range(a + 1, 4):
                z[a] = z[a] - low[c][a] * z[c]

        def pick(which):
            columns = []
            for c in range(4):
                value = jnp.sum(jnp.where((lanes == which) & (sub < 3), z[c], 0.0), axis=1, keepdims=True)
                columns.append(jnp.broadcast_to(value, (8, BLOCK)))
            return columns

        own_pose = pick(1)
        if not last:
            low_pose, up_pose = pick(0), pick(2)
            prepare(own_pose, low_pose, up_pose)
        wait_rows(line_in.at[it], lines - 3, line_recv.at[it])
        totals = jnp.sum(line_in[it], axis=0)
        spread = (totals[:, 28:29] + PRIOR_TOP) / (3.0 * totals[:, 27:28] + 1.0)
        spread = jnp.broadcast_to(spread, (8, BLOCK))
        wait_rows(line_in.at[it], lines - 1, line_send.at[it])

    line = jnp.zeros((8, BLOCK), F32)
    for c in range(4):
        lane = 3 * sub + c if c < 3 else 9 + sub
        line = line + jnp.where((lanes == lane) & (sub < 3), own_pose[c], 0.0)
    fitted[...] = jnp.sum(line, axis=0, keepdims=True)[:, 0:12]
    final_spread[...] = spread[0:1, 0:1]


def em(src, near, near_pose, pose, cells, lines, segs):
    blocks = src.shape[0]
    vmem = pl.BlockSpec(memory_space=pltpu.VMEM)
    smem = pl.BlockSpec(memory_space=pltpu.SMEM)
    return pl.pallas_call(
        functools.partial(em_kernel, lines, segs),
        out_shape=(
            jax.ShapeDtypeStruct((5, 2, blocks // 2 * BLOCK), F32),
            jax.ShapeDtypeStruct((1, 12), F32),
            jax.ShapeDtypeStruct((1, 1), F32),
        ),
        in_specs=[vmem, vmem, vmem, vmem, smem],
        out_specs=(vmem, vmem, vmem),
        scratch_shapes=[
            pltpu.VMEM((2 * NCELL, 64, CT), jnp.bfloat16),
            pltpu.VMEM((blocks, BLOCK, 64), jnp.bfloat16),
            pltpu.VMEM((2 * NCELL, 8, BLOCK), F32),
            pltpu.VMEM((UNROLL, BLOCK, 2 * CT), jnp.bfloat16),
            pltpu.VMEM((UNROLL, BLOCK, BLOCK), F32),
            pltpu.VMEM((ITERS, 1, BLOCK), F32),
            pltpu.VMEM((ITERS, 1, BLOCK), F32),
            pltpu.VMEM((ITERS, segs, 1, BLOCK), F32),
            pltpu.VMEM((ITERS, lines, 1, BLOCK), F32),
            pltpu.SemaphoreType.DMA((ITERS,)),
            pltpu.SemaphoreType.DMA((ITERS,)),
            pltpu.SemaphoreType.DMA((ITERS,)),
            pltpu.SemaphoreType.DMA((ITERS, 2)),
            pltpu.SemaphoreType.DMA((ITERS,)),
        ],
        compiler_params=pltpu.CompilerParams(
            collective_id=1, has_side_effects=True, vmem_limit_bytes=VMEM_LIMIT
        ),
        name="em",
    )(src, near, near_pose, pose, cells)


def solution(mesh):
    lines, segs = mesh.shape["line"], mesh.shape["seg"]

    def on_device(points, rows, cells, pose):
        tiled = points.reshape(points.shape[2], points.shape[3] // BLOCK, BLOCK)
        pose_row = pose.reshape(1, 12)
        near, near_pose, src = fetch(tiled, rows[0, 0], pose_row, lines)
        matched, fitted, spread = em(src, near, near_pose, pose_row, cells[0, 0], lines, segs)
        return jnp.transpose(matched, (1, 0, 2))[None, None], fitted.reshape(12, 1), spread.reshape(1)

    return jax.shard_map(
        on_device,
        mesh=mesh,
        in_specs=(
            P("line", "seg", None, None),
            P("line", "seg", None, None),
            P("line", "seg", None, None),
            P(None, "line"),
        ),
        out_specs=(P("line", "seg", None, None, None), P(None, "line"), P()),
        check_vma=False,
    )
```

time: 101 us -> 73.4 us (0.73)
  Pallas kernels: 92.7 us -> 66.6 us
  local copies, waits for them, and re-layouts: 5.66 us -> 4.22 us
    pallas_call x1, Pallas kernels: 78.1 us -> 56.6 us  [em(): pl.pallas_call(functools.partial(em_kernel, lines, segs), out_shape=(jax....]
    pallas_call x1, Pallas kernels: 14.6 us -> 9.97 us  [fetch(): pl.pallas_call(functools.partial(fetch_kernel, lines), out_shape=(jax.Sha...]
    unnamed x8 -> x10, local copies, waits for them, and re-layouts: 5.66 us -> 4.22 us
where the time goes in v2:
time: 73.4 us; the launch traced here: 73.2 us
  Pallas kernels  66.6 us (91%)
  local copies, waits for them, and re-layouts  4.22 us (6%)
  between operations  2.35 us (3%)
    pallas_call x1, Pallas kernels, em(): pl.pallas_call(functools.partial(em_kernel, lines, segs), out_shape=(jax....  56.6 us
    pallas_call x1, Pallas kernels, fetch(): pl.pallas_call(functools.partial(fetch_kernel, lines), out_shape=(jax.Sha...  9.97 us
    unnamed x10, local copies, waits for them, and re-layouts  4.22 us

profile of v2, /device:TPU:1, one launch (start us, length us, event | category | flops | bytes accessed | tf_op | source)
XLA Modules:
  0.0 73.2 jit_solution(17579347419720057070)
XLA Ops:
  0.6 0.0 copy-start.2
  0.6 0.6 copy-done.2
  1.3 0.0 copy-start
  1.3 1.0 %copy-done = f32[1,1,3,32768]{3,1,2,0:T(1,128)S(1)} copy-done((f32[1,1,3,32768]{3,1,2,0:T(1,128)S(1)}, f32[1,1,3,32768]{3,1,2,0:T(1,128)}, u32[]{:S(2)}) %copy-start) | copy-done | bytes 393240
  2.3 0.0 copy-start.1
  2.3 0.7 %copy-done.1 = s32[1,1,2,3072]{3,2,1,0:T(2,128)S(1)} copy-done((s32[1,1,2,3072]{3,2,1,0:T(2,128)S(1)}, s32[1,1,2,3072]{3,2,1,0:T(2,128)}, u32[]{:S(2)}) %copy-start.1) | copy-done | bytes 24600
  3.0 10.0 %fetch.1 = (f32[2,3,64,128]{3,2,1,0:T(8,128)S(1)}, f32[2,1,12]{2,1,0:T(1,128)S(1)}, f32[48,8,128]{2,1,0:T(8,128)S(1)}) custom-call(f32[3,256,128]{2,1,0:T(8,128)S(1)} %bitcast.9, s32[2,3072]{1,0:T(2,128)S(1)} %bitcast.11, f32[1,12]{1,0:T(1,128)S(1)} %bitcast.12), custom_call_target="tpu_custom_call" | custom-call | tf_op jit(solution)/shard_map/fetch/pallas_call | solution.py:106
  13.0 0.0 copy-start.3
  13.0 0.7 copy-done.3
  13.7 56.6 %em.1 = (f32[5,2,3072]{2,1,0:T(2,128)S(1)}, f32[1,12]{1,0:T(1,128)S(1)}, f32[1,1]{1,0:T(1,128)}) custom-call(f32[48,8,128]{2,1,0:T(8,128)S(1)} %get-tuple-element.9.src, f32[2,3,64,128]{3,2,1,0:T(8,128)S(1)} %get-tuple-element.10.near, f32[2,1,12]{2,1,0:T(1,128)S(1)} %get-tuple-element.11.near_pose, f32[1,12]{1,0:T(1,128)S(1)} %bitcast.13, s32[2,24]{1,0:T(2,128)S(1)} %bitcast.14), custom_call_target="tpu_custom_call" | custom-call | tf_op jit(solution)/shard_map/em/pallas_call | solution.py:419
  70.3 0.7 copy.10
  71.0 0.5 copy.11
Async XLA Ops:
  0.6 0.7 copy-start.2
  1.3 1.0 %copy-start = (f32[1,1,3,32768]{3,1,2,0:T(1,128)S(1)}, f32[1,1,3,32768]{3,1,2,0:T(1,128)}, u32[]{:S(2)}) copy-start(f32[1,1,3,32768]{3,1,2,0:T(1,128)} %param.4) | copy-start | bytes 1179652
  2.3 0.7 %copy-start.1 = (s32[1,1,2,3072]{3,2,1,0:T(2,128)S(1)}, s32[1,1,2,3072]{3,2,1,0:T(2,128)}, u32[]{:S(2)}) copy-start(s32[1,1,2,3072]{3,2,1,0:T(2,128)} %param.5) | copy-start | bytes 73732
  13.0 0.7 copy-start.3

commit v3 on v2

--- a/solution.py
+++ b/solution.py
@@ -17,8 +17,8 @@
 LOG2E = math.log2(math.e)
 MARGIN = NCELL * CT
 CHUNK = 16
-UNROLL = 8
-GATHER = 4
+UNROLL = 24
+GATHER = 8
 VMEM_LIMIT = 16 << 20
 MESH = pl.DeviceIdType.MESH
 F32 = jnp.float32
@@ -28,13 +28,15 @@
     return lax.broadcasted_iota(jnp.int32, shape, dim)
 
 
-def fetch_kernel(lines, points, rows, pose, near, near_pose, src, own, own_sem, send_sem, recv_sem):
+def fetch_kernel(lines, points, row_lists, pose, near, near_pose, src, own, rows, own_sem, send_sem, recv_sem):
     me = lax.axis_index("line")
     upper, lower = lax.rem(me + 1, lines), lax.rem(me + lines - 1, lines)
     tiles = points.shape[1]
     margin_tiles = MARGIN // BLOCK
     low_tiles = pl.ds(0, margin_tiles)
     high_tiles = pl.ds(tiles - margin_tiles, margin_tiles)
+
+    has_lower, has_upper = me > 0, me < lines - 1
 
     barrier = pltpu.get_barrier_semaphore()
     for peer in (lower, upper):
@@ -43,6 +45,8 @@
         pltpu.make_async_copy(points.at[:, part], own.at[d], own_sem.at[d])
         for d, part in enumerate((low_tiles, high_tiles))
     ]
+    row_copy = pltpu.make_async_copy(row_lists, rows, own_sem.at[2])
+    row_copy.start()
     for copy in locals_:
         copy.start()
 
@@ -56,12 +60,22 @@
             device_id_type=MESH,
         )
 
-    sends = [
+    up = [
         remote(points.at[:, high_tiles], near.at[0], 0, upper),
+        remote(pose, near_pose.at[0], 2, upper),
+    ]
+    down = [
         remote(points.at[:, low_tiles], near.at[1], 1, lower),
-        remote(pose, near_pose.at[0], 2, upper),
         remote(pose, near_pose.at[1], 3, lower),
     ]
+
+    for side, there in enumerate((has_lower, has_upper)):
+
+        @pl.when(jnp.logical_not(there))
+        def _():
+            near[side] = jnp.zeros_like(near[side])
+            near_pose[side] = jnp.zeros_like(near_pose[side])
+
     sub = iota((8, BLOCK), 0)
     blocks = rows.shape[1] // BLOCK
 
@@ -91,13 +105,26 @@
                 src[d * blocks + b] = value
 
     pl.semaphore_wait(barrier, 2)
-    for copy in sends:
-        copy.start()
+
+    for there, copies in ((has_upper, up), (has_lower, down)):
+
+        @pl.when(there)
+        def _():
+            for copy in copies:
+                copy.start()
+
+    row_copy.wait()
     for d in range(2):
         locals_[d].wait()
         gather(d)
-    for copy in sends:
-        copy.wait()
+    for there, sent, received in ((has_upper, up, down), (has_lower, down, up)):
+
+        @pl.when(there)
+        def _():
+            for copy in sent:
+                copy.wait_send()
+            for copy in received:
+                copy.wait_recv()
 
 
 def fetch(points, rows, pose, lines):
@@ -110,11 +137,12 @@
             jax.ShapeDtypeStruct((2, 1, 12), F32),
             jax.ShapeDtypeStruct((blocks, 8, BLOCK), F32),
         ),
-        in_specs=[pl.BlockSpec(memory_space=pl.ANY), vmem, vmem],
+        in_specs=[pl.BlockSpec(memory_space=pltpu.HBM)] * 3,
         out_specs=(vmem, vmem, vmem),
         scratch_shapes=[
             pltpu.VMEM((2, 3, MARGIN // BLOCK, BLOCK), F32),
-            pltpu.SemaphoreType.DMA((2,)),
+            pltpu.VMEM(rows.shape, jnp.int32),
+            pltpu.SemaphoreType.DMA((3,)),
             pltpu.SemaphoreType.DMA((4,)),
             pltpu.SemaphoreType.DMA((4,)),
         ],
@@ -170,8 +198,8 @@
 
 
 def em_kernel(
-    lines, segs, src, near, near_pose, pose, cells, matched, fitted, final_spread,
-    side_y, side_m, centres, weights, energies, row_out, line_out, seg_in, line_in,
+    lines, segs, src, near, near_pose, pose_in, cells_in, matched, fitted, final_spread,
+    pose, cells, load_sem, side_y, side_m, centres, weights, energies, row_out, line_out, seg_in, line_in,
     seg_send, seg_recv, line_send, near_recv, line_recv,
 ):
     my_line, my_seg = lax.axis_index("line"), lax.axis_index("seg")
@@ -182,14 +210,17 @@
 
     barrier = pltpu.get_barrier_semaphore()
 
-    @pl.loop(1, segs)
-    def _(k):
+    loads = [
+        pltpu.make_async_copy(pose_in, pose, load_sem.at[0]),
+        pltpu.make_async_copy(cells_in, cells, load_sem.at[1]),
+    ]
+    for copy in loads:
+        copy.start()
+    for k in range(1, segs):
         pl.semaphore_signal(
             barrier, inc=1, device_id={"seg": lax.rem(my_seg + k, segs)}, device_id_type=MESH
         )
-
-    @pl.loop(1, lines)
-    def _(k):
+    for k in range(1, lines):
         pl.semaphore_signal(
             barrier, inc=1, device_id={"line": lax.rem(my_line + k, lines)}, device_id_type=MESH
         )
@@ -228,12 +259,11 @@
 
     lower, upper = lax.rem(my_line + lines - 1, lines), lax.rem(my_line + 1, lines)
 
-    own_pose = pose_columns(pose[...])
     low_pose = pose_columns(near_pose[0])
     up_pose = pose_columns(near_pose[1])
     spread = jnp.full((8, BLOCK), SPREAD_START, F32)
 
-    def prepare(own_pose, low_pose, up_pose):
+    def prepare_targets(low_pose, up_pose):
         for d in range(2):
 
             @pl.loop(0, NCELL)
@@ -253,6 +283,7 @@
                     value = operand(world[t] - centre, False)
                     side_y[d * NCELL + c, :, here] = value.astype(jnp.bfloat16)
 
+    def prepare_sources(own_pose):
         for d in range(2):
 
             @pl.loop(0, blocks // UNROLL)
@@ -265,7 +296,11 @@
                     value = operand(moved - centres[cell], True)
                     side_m[d * blocks + b] = jnp.transpose(value).astype(jnp.bfloat16)
 
-    prepare(own_pose, low_pose, up_pose)
+    prepare_targets(low_pose, up_pose)
+    for copy in loads:
+        copy.wait()
+    own_pose = pose_columns(pose[...])
+    prepare_sources(own_pose)
     for it in range(ITERS):
         last = it == ITERS - 1
         rate = LOG2E / (2.0 * spread)
@@ -289,16 +324,17 @@
                         energy = energy + part[:, t * BLOCK : (t + 1) * BLOCK]
                     energies[u, here, :] = energy
                     high = weight.astype(jnp.bfloat16)
-                    weights[u, here, 0:CT] = high
-                    weights[u, here, CT : 2 * CT] = (weight - high.astype(F32)).astype(jnp.bfloat16)
-                values = side_y[cell, 0:32, :]
+                    weights[u, here, :] = high
+                    weights[u, BLOCK + i * CHUNK : BLOCK + (i + 1) * CHUNK, :] = (
+                        weight - high.astype(F32)
+                    ).astype(jnp.bfloat16)
                 out = lax.dot_general(
                     weights[u],
-                    jnp.concatenate([values, values], axis=1),
+                    side_y[cell, 0:32, :],
                     (((1,), (1,)), ((), ())),
                     preferred_element_type=F32,
                 )
-                out = jnp.transpose(out)
+                out = jnp.transpose(out[:BLOCK] + out[BLOCK:])
                 pulled = out[0:8] + jnp.where(sub == 3, 0.0, out[8:16] + out[16:24])
                 energy = jnp.sum(jnp.transpose(energies[u]), axis=0, keepdims=True)
                 total = jnp.broadcast_to(pulled[3:4], (8, BLOCK))
@@ -397,7 +433,8 @@
         own_pose = pick(1)
         if not last:
             low_pose, up_pose = pick(0), pick(2)
-            prepare(own_pose, low_pose, up_pose)
+            prepare_targets(low_pose, up_pose)
+            prepare_sources(own_pose)
         wait_rows(line_in.at[it], lines - 3, line_recv.at[it])
         totals = jnp.sum(line_in[it], axis=0)
         spread = (totals[:, 28:29] + PRIOR_TOP) / (3.0 * totals[:, 27:28] + 1.0)
@@ -415,7 +452,7 @@
 def em(src, near, near_pose, pose, cells, lines, segs):
     blocks = src.shape[0]
     vmem = pl.BlockSpec(memory_space=pltpu.VMEM)
-    smem = pl.BlockSpec(memory_space=pltpu.SMEM)
+    hbm = pl.BlockSpec(memory_space=pltpu.HBM)
     return pl.pallas_call(
         functools.partial(em_kernel, lines, segs),
         out_shape=(
@@ -423,13 +460,16 @@
             jax.ShapeDtypeStruct((1, 12), F32),
             jax.ShapeDtypeStruct((1, 1), F32),
         ),
-        in_specs=[vmem, vmem, vmem, vmem, smem],
+        in_specs=[vmem, vmem, vmem, hbm, hbm],
         out_specs=(vmem, vmem, vmem),
         scratch_shapes=[
+            pltpu.VMEM(pose.shape, F32),
+            pltpu.SMEM(cells.shape, jnp.int32),
+            pltpu.SemaphoreType.DMA((2,)),
             pltpu.VMEM((2 * NCELL, 64, CT), jnp.bfloat16),
             pltpu.VMEM((blocks, BLOCK, 64), jnp.bfloat16),
             pltpu.VMEM((2 * NCELL, 8, BLOCK), F32),
-            pltpu.VMEM((UNROLL, BLOCK, 2 * CT), jnp.bfloat16),
+            pltpu.VMEM((UNROLL, 2 * BLOCK, CT), jnp.bfloat16),
             pltpu.VMEM((UNROLL, BLOCK, BLOCK), F32),
             pltpu.VMEM((ITERS, 1, BLOCK), F32),
             pltpu.VMEM((ITERS, 1, BLOCK), F32),
@@ -454,8 +494,12 @@
     def on_device(points, rows, cells, pose):
         tiled = points.reshape(points.shape[2], points.shape[3] // BLOCK, BLOCK)
         pose_row = pose.reshape(1, 12)
-        near, near_pose, src = fetch(tiled, rows[0, 0], pose_row, lines)
-        matched, fitted, spread = em(src, near, near_pose, pose_row, cells[0, 0], lines, segs)
+        tiled, row_lists, pose_row, cell_lists = (
+            pltpu.with_memory_space_constraint(value, pltpu.HBM)
+            for value in (tiled, rows[0, 0], pose_row, cells[0, 0])
+        )
+        near, near_pose, src = fetch(tiled, row_lists, pose_row, lines)
+        matched, fitted, spread = em(src, near, near_pose, pose_row, cell_lists, lines, segs)
         return jnp.transpose(matched, (1, 0, 2))[None, None], fitted.reshape(12, 1), spread.reshape(1)
 
     return jax.shard_map(

time: 73.4 us -> 66.8 us (0.910)
  Pallas kernels: 66.6 us -> 63.1 us
  local copies, waits for them, and re-layouts: 4.22 us -> 1.16 us
    pallas_call x1, Pallas kernels: 56.6 us -> 53.4 us  [em(): pl.pallas_call(functools.partial(em_kernel, lines, segs), out_shape=(jax....]
    unnamed x10 -> x2, local copies, waits for them, and re-layouts: 4.22 us -> 1.16 us
where the time goes in v3:
time: 66.8 us; the launch traced here: 66.6 us
  Pallas kernels  63.1 us (94%)
  between operations  2.41 us (4%)
  local copies, waits for them, and re-layouts  1.16 us (2%)
    pallas_call x1, Pallas kernels, em(): pl.pallas_call(functools.partial(em_kernel, lines, segs), out_shape=(jax....  53.4 us
    pallas_call x1, Pallas kernels, fetch(): pl.pallas_call(functools.partial(fetch_kernel, lines), out_shape=(jax.Sha...  9.62 us

profile of v3, /device:TPU:1, one launch (start us, length us, event | category | flops | bytes accessed | tf_op | source)
XLA Modules:
  0.0 66.6 jit_solution(5825270690190904068)
XLA Ops:
  0.6 9.6 %fetch.1 = (f32[2,3,64,128]{3,2,1,0:T(8,128)S(1)}, f32[2,1,12]{2,1,0:T(1,128)S(1)}, f32[48,8,128]{2,1,0:T(8,128)S(1)}) custom-call(f32[3,256,128]{2,1,0:T(8,128)} %bitcast.11, s32[2,3072]{1,0:T(2,128)} %bitcast.12, f32[1,12]{1,0:T(1,128)} %bitcast.13), custom_call_target="tpu_custom_call" | custom-call | tf_op jit(solution)/shard_map/fetch/pallas_call | solution.py:133
  10.3 53.4 %em.1 = (f32[5,2,3072]{2,1,0:T(2,128)S(1)}, f32[1,12]{1,0:T(1,128)S(1)}, f32[1,1]{1,0:T(1,128)}) custom-call(f32[48,8,128]{2,1,0:T(8,128)S(1)} %get-tuple-element.9.src, f32[2,3,64,128]{3,2,1,0:T(8,128)S(1)} %get-tuple-element.10.near, f32[2,1,12]{2,1,0:T(1,128)S(1)} %get-tuple-element.11.near_pose, f32[1,12]{1,0:T(1,128)} %bitcast.14, s32[2,24]{1,0:T(2,128)} %bitcast.15), custom_call_target="tpu_custom_call" | custom-call | tf_op jit(solution)/shard_map/em/pallas_call | solution.py:456
  63.7 0.7 copy.10
  64.4 0.5 copy.11
